TPU v7x, 32 devices: a whole 2x2x4 slice. The times are simulated.
32 devices in a mesh: grp: 4 (over x, core), seq: 8 (over z, y).
Axes of the slice: x: 2, y: 2, z: 4, core: 2. Of those that a mesh axis runs over, the one named last changes fastest.
Arguments:
- queries: bfloat16 [12288, 4096], P(('grp', 'seq')), may hold values from -6 to 6
- keys: bfloat16 [12288, 4096], P(('grp', 'seq')), may hold values from -6 to 6
- values: bfloat16 [12288, 4096], P(('grp', 'seq')), may hold values from -6 to 6
- gain: bfloat16 [4096], replicated, may hold values from 0.5 to 1.5
Outputs:
- attended: bfloat16 [12288, 4096], P(('grp', 'seq'))
All inputs are finite; a program needn't handle non-finite values.
Results may differ from a plain program's by a relative error of at most 0.0053.
Values sent between devices are 32-bit elements; how exact they have to be, the bound alone decides.
No kernel may reach another device: no remote copies, remote signals or barrier semaphores. Data moves between devices by JAX's collectives and lax.ppermute only.
A program may use at most 256 MiB of HBM per device.

v0:
```python
import jax
import jax.numpy as jnp
from jax import lax
from jax.sharding import PartitionSpec as P

HEADS = 32
HEAD_DIM = 128


def entering(value, axis, join, neutral):
    count, mine = (lax.axis_size(axis), lax.axis_index(axis))
    pieces = lax.all_gather(value, axis)
    subtotal = jnp.full_like(value, 0) + jnp.asarray(neutral, value.dtype)

    def lap(position, subtotal):
        longer = join(subtotal, pieces[position])
        return jnp.where(position < mine, longer, subtotal)

    return lax.fori_loop(0, count - 1, lap, subtotal)


def combine_sum(earlier, later):
    return earlier + later


def shards(queries, keys, values, gain):
    rows = queries.shape[0]
    fq = (
        jax.nn.silu(queries.astype(jnp.float32)).astype(jnp.bfloat16).reshape(rows, HEADS, HEAD_DIM)
    )
    fk = jax.nn.silu(keys.astype(jnp.float32)).astype(jnp.bfloat16).reshape(rows, HEADS, HEAD_DIM)
    vals = values.reshape(rows, HEADS, HEAD_DIM)
    local = jnp.einsum("thd,the->hde", fk, vals, preferred_element_type=jnp.float32)
    empty = jnp.zeros((HEADS, HEAD_DIM, HEAD_DIM), jnp.float32)
    within = entering(local, "seq", combine_sum, empty)
    total = lax.psum(local, "seq")
    before = entering(total, "grp", combine_sum, empty)
    carried = before + within
    positions = jnp.arange(rows, dtype=jnp.int32)
    causal = positions[:, None] >= positions[None, :]
    scores = jnp.einsum("thd,shd->hts", fq, fk, preferred_element_type=jnp.float32)
    scores = jnp.where(causal[None], scores, 0.0).astype(jnp.bfloat16)
    intra = jnp.einsum("hts,she->the", scores, vals, preferred_element_type=jnp.float32)
    inter = jnp.einsum(
        "thd,hde->the", fq, carried.astype(jnp.bfloat16), preferred_element_type=jnp.float32
    )
    mixed = intra + inter
    meansq = jnp.mean(mixed * mixed, axis=-1, keepdims=True)
    gains = gain.astype(jnp.float32).reshape(HEADS, HEAD_DIM)
    normed = mixed * lax.rsqrt(meansq + 1e-06) * gains[None]
    return normed.reshape(rows, HEADS * HEAD_DIM).astype(jnp.bfloat16)


def solution(mesh):
    return jax.shard_map(
        shards,
        mesh=mesh,
        in_specs=(P(("grp", "seq"), None), P(("grp", "seq"), None), P(("grp", "seq"), None), P()),
        out_specs=P(("grp", "seq"), None),
        check_vma=False,
    )
```

profile of v0, /device:TPU:0, one launch (start us, length us, event | category | flops | bytes accessed | tf_op | source)
XLA Modules:
  0.0 443.5 jit_solution(8854764190640074062)
XLA Ops:
  6.5 0.0 copy-start
  6.5 5.5 %fusion.10 = bf16[384,4096]{1,0:T(8,128)(2,1)} fusion(bf16[384,4096]{1,0:T(8,128)(2,1)} %param.9), kind=kLoop, calls=%fused_computation.17 | loop fusion | flops 9437184 | bytes 6291456 | tf_op jit(solution)/shard_map/convert_element_type | solution.py:31
  12.0 4.7 %copy.18 = bf16[384,4096]{0,1:T(8,128)(2,1)} copy(bf16[384,4096]{1,0:T(8,128)(2,1)} %fusion.10) | data formatting | bytes 6291456 | tf_op jit(solution)/shard_map/reshape | solution.py:31
  16.7 0.0 copy-done
  16.7 4.2 fusion.15
  20.9 0.0 all-gather.6.cloned.1.call-update
  21.0 230.2 %all-gather.6.cloned.1.call-done = f32[256,128,128]{2,1,0:T(8,128)} async-done(((f32[32,128,128]{2,1,0:T(8,128)}), f32[256,128,128]{2,1,0:T(8,128)}) %all-gather.6.cloned.1.call-update) | async-done | bytes 16777232 | tf_op jit(solution)/shard_map/all_gather | solution.py:12
  251.1 0.7 all-reduce.2.cloned.1.call-update
  251.9 0.0 all-gather.4.cloned.1.call-start
  251.9 104.1 %all-reduce.2.cloned.1.call-done = f32[1,32,128,128]{3,2,1,0:T(8,128)} async-done(((f32[1,32,128,128]{3,2,1,0:T(8,128)}), f32[1,32,128,128]{3,2,1,0:T(8,128)}) %all-reduce.2.cloned.1.call-update) | async-done | bytes 2097168 | tf_op jit(solution)/shard_map/psum | solution.py:36
  356.0 0.0 all-gather.4.cloned.1.call-update
  356.1 0.0 copy-done.3
  356.2 9.2 %fusion = f32[32,384,128]{1,2,0:T(8,128)} fusion(pred[384,384]{1,0:T(8,128)(4,1)S(1)} %iota_compare_fusion, bf16[384,32,128]{0,2,1:T(8,128)(2,1)} %bitcast.58, bf16[384,4096]{1,0:T(8,128)(2,1)S(1)} %copy-done, bf16[384,4096]{1,0:T(8,128)(2,1)} %param.8), kind=kOutput, calls=%fused_computation.3 | convolution fusion | flops 2434793472 | bytes 15876096 | tf_op jit(solution)/shard_map/hts,she->the/dot_general | solution.py:43
  365.4 28.6 %while.29 = (s32[]{:T(128)}, f32[32,128,128]{2,1,0:T(8,128)}, s32[]{:T(128)}, f32[8,32,128,128]{3,2,1,0:T(8,128)}, s32[]{:T(128)}, /*index=5*/s32[]{:T(128)}) while((s32[]{:T(128)}, f32[32,128,128]{2,1,0:T(8,128)}, s32[]{:T(128)}, f32[8,32,128,128]{3,2,1,0:T(8,128)}, s32[]{:T(128)}, /*index=5*/s32[]{:T(128)}) %tuple.73), condition=%wide.region_4.5_spmd.clone, body=%wide.region_3.4_spmd.clone.sunk | while | flops 1572868 | bytes 6291557 | solution.py:19
  365.4 3.9 add_select_fusion.5
  369.3 4.2 add_select_fusion.5
  373.5 4.1 add_select_fusion.5
  377.6 4.1 add_select_fusion.5
  381.7 4.1 add_select_fusion.5
  385.7 4.2 add_select_fusion.5
  389.9 4.1 add_select_fusion.5
  394.0 21.2 %all-gather.4.cloned.1.call-done = f32[4,32,128,128]{3,2,1,0:T(8,128)} async-done(((f32[1,32,128,128]{3,2,1,0:T(8,128)}), f32[4,32,128,128]{3,2,1,0:T(8,128)}) %all-gather.4.cloned.1.call-update) | async-done | bytes 8388624 | tf_op jit(solution)/shard_map/all_gather | solution.py:12
  415.2 7.0 %while.28 = (s32[]{:T(128)}, f32[32,128,128]{2,1,0:T(8,128)S(1)}, s32[]{:T(128)}, f32[4,32,128,128]{3,2,1,0:T(8,128)}, s32[]{:T(128)}, /*index=5*/s32[]{:T(128)}) while((s32[]{:T(128)}, f32[32,128,128]{2,1,0:T(8,128)S(1)}, s32[]{:T(128)}, f32[4,32,128,128]{3,2,1,0:T(8,128)}, s32[]{:T(128)}, /*index=5*/s32[]{:T(128)}) %tuple.72), condition=%wide.region_2.3_spmd.clone, body=%wide.region_1.2_spmd.clone.sunk | while | flops 1572868 | bytes 6291557 | solution.py:19
  415.2 2.3 add_select_fusion.4
  417.5 2.3 add_select_fusion.4
  419.9 2.3 add_select_fusion.4
  422.2 0.0 slice-start
  422.2 0.0 slice-start.1
  422.2 7.4 %multiply_reduce_fusion = (f32[384,32]{0,1:T(8,128)S(1)}, f32[32,128,384]{2,1,0:T(8,128)S(1)}) fusion(f32[32,384,128]{1,2,0:T(8,128)} %fusion, f32[32,128,128]{2,1,0:T(8,128)S(1)} %get-tuple-element.163, f32[32,128,128]{2,1,0:T(8,128)} %get-tuple-element.164, bf16[384,4096]{1,0:T(8,128)(2,1)} %param.8), kind=kOutput, calls=%fused_computation.20 | convolution fusion | flops 417845248 | bytes 19972096 | tf_op jit(solution)/shard_map/thd,hde->the/dot_general | solution.py:44
  429.7 2.5 multiply_convert_fusion
  432.2 4.8 %copy.16 = bf16[384,4096]{1,0:T(8,128)(2,1)} copy(bf16[384,4096]{0,1:T(8,128)(2,1)} %bitcast.59) | data formatting | bytes 6291456 | tf_op jit(solution)/shard_map/convert_element_type | solution.py:51
  437.0 0.0 copy-done.1
  (14 shorter events, 0.1 us)
Async XLA Ops:
  6.5 10.2 %copy-start = (bf16[384,4096]{1,0:T(8,128)(2,1)S(1)}, bf16[384,4096]{1,0:T(8,128)(2,1)}, u32[]{:S(2)}) copy-start(bf16[384,4096]{1,0:T(8,128)(2,1)} %param.10) | copy-start | bytes 9437188
  6.5 244.6 %all-gather.6.cloned.1.call-start = ((), (), s32[]{:S(2)}) async-start(), calls=%async_computation.2 | async-start | bytes 18874368 | tf_op jit(solution)/shard_map/all_gather | solution.py:12
  20.9 335.2 %copy-start.3 = (bf16[4096]{0:T(1024)(128)(2,1)S(1)}, bf16[4096]{0:T(1024)(128)(2,1)}, u32[]{:S(2)}) copy-start(bf16[4096]{0:T(1024)(128)(2,1)} %param.11) | copy-start | bytes 24580
  251.1 104.9 %all-reduce.2.cloned.1.call-start = ((), (), s32[]{:S(2)}) async-start(), calls=%async_computation | async-start | bytes 4194304 | tf_op jit(solution)/shard_map/psum | solution.py:36
  251.9 163.3 %all-gather.4.cloned.1.call-start = ((), (), s32[]{:S(2)}) async-start(), calls=%async_computation.1 | async-start | bytes 10485760 | tf_op jit(solution)/shard_map/all_gather | solution.py:12
  365.4 49.8 %copy-start.2 = (f32[32,128,128]{2,1,0:T(8,128)S(1)}, f32[32,128,128]{2,1,0:T(8,128)}, u32[]{:S(2)}) copy-start(f32[32,128,128]{2,1,0:T(8,128)} %custom-call) | copy-start | bytes 6291460
  422.2 7.5 %slice-start = ((s8[6291456]{0:T(1024)(128)(4,1)}), s8[4194304]{0:T(1024)(128)(4,1)S(1)}, s32[]{:S(2)}) async-start(s8[6291456]{0:T(1024)(128)(4,1)} %bitcast.61), calls=%async_computation.3 | async-start | bytes 8388608
  422.2 7.5 %slice-start.1 = ((s8[6291456]{0:T(1024)(128)(4,1)}), s8[2097152]{0:T(1024)(128)(4,1)S(1)}, s32[]{:S(2)}) async-start(s8[6291456]{0:T(1024)(128)(4,1)} %bitcast.61), calls=%async_computation.4 | async-start | bytes 4194304
  432.2 4.8 %copy-start.1 = (bf16[384,4096]{1,0:T(8,128)(2,1)S(1)}, bf16[384,4096]{1,0:T(8,128)(2,1)}, u32[]{:S(2)}) copy-start(bf16[384,4096]{1,0:T(8,128)(2,1)} %param.10) | copy-start | bytes 9437188
Sparse Core Ops, SparseCore 0:
  21.1 229.9 all-gather.5
  255.6 100.4 all-reduce.1
  357.6 57.5 all-gather.3
where the time goes:
time: 444 us; the launch traced here: 443 us
  waiting for transfers between devices  356 us (80%)
  other arithmetic  43.6 us (10%)
  matrix products  20.9 us (5%)
  between operations  13.2 us (3%)
  local copies, waits for them, and re-layouts  9.5 us (2%)
    all_gather x2, waiting for transfers between devices, entering(): pieces = lax.all_gather(value, axis)  251 us
    psum x1, waiting for transfers between devices, shards(): total = lax.psum(local, 'seq')  104 us
    select_n x10, other arithmetic, lap(): return jnp.where(position < mine, longer, subtotal)  35.5 us
    dot_general x1, matrix products, shards(): jnp.einsum('hts,she->the', scores, vals, preferred_element_type=jnp.float32)  9.23 us
  transfers between devices with their start and end apart: 3, of which 3 were waited for; matrix products, arithmetic and copies ran while one was open for 9% of the time, Pallas kernels for 0%

commit v1 on v0

--- a/solution.py
+++ b/solution.py
@@ -33,7 +33,7 @@
     local = jnp.einsum("thd,the->hde", fk, vals, preferred_element_type=jnp.float32)
     empty = jnp.zeros((HEADS, HEAD_DIM, HEAD_DIM), jnp.float32)
     within = entering(local, "seq", combine_sum, empty)
-    total = lax.psum(local, "seq")
+    total = jnp.sum(lax.all_gather(local, "seq"), axis=0)
     before = entering(total, "grp", combine_sum, empty)
     carried = before + within
     positions = jnp.arange(rows, dtype=jnp.int32)

time: 444 us -> 346 us (0.78)
  waiting for transfers between devices: 356 us -> 249 us
  other arithmetic: 43.6 us -> 52.8 us
    all_gather x2 -> x1, waiting for transfers between devices: 251 us -> 18.6 us  [entering(): pieces = lax.all_gather(value, axis)]
    all_gather x0 -> x1, waiting for transfers between devices: none -> 230 us  [shards(): total = jnp.sum(lax.all_gather(local, 'seq'), axis=0)]
    psum x1 -> x0, waiting for transfers between devices: 104 us -> none  [shards(): total = lax.psum(local, 'seq')]
    reduce_sum x0 -> x1, other arithmetic: none -> 9.09 us  [shards(): total = jnp.sum(lax.all_gather(local, 'seq'), axis=0)]
  transfers between devices with their start and end apart: 3 -> 2, of which waited for: 3 -> 2; matrix products, arithmetic and copies ran while one was open for 9% -> 11% of each run, Pallas kernels for 0% -> 0%
where the time goes in v1:
time: 346 us; the launch traced here: 345 us
  waiting for transfers between devices  249 us (72%)
  other arithmetic  52.8 us (15%)
  matrix products  20.9 us (6%)
  between operations  13.5 us (4%)
  local copies, waits for them, and re-layouts  9.47 us (3%)
    all_gather x1, waiting for transfers between devices, shards(): total = jnp.sum(lax.all_gather(local, 'seq'), axis=0)  230 us
    select_n x10, other arithmetic, lap(): return jnp.where(position < mine, longer, subtotal)  35.6 us
    all_gather x1, waiting for transfers between devices, entering(): pieces = lax.all_gather(value, axis)  18.6 us
    dot_general x1, matrix products, shards(): jnp.einsum('hts,she->the', scores, vals, preferred_element_type=jnp.float32)  9.22 us
    reduce_sum x1, other arithmetic, shards(): total = jnp.sum(lax.all_gather(local, 'seq'), axis=0)  9.09 us
    dot_general x1, matrix products, shards(): jnp.einsum('thd,hde->the', fq, carried.astype(jnp.bfloat16), preferred_el...  7.44 us
  transfers between devices with their start and end apart: 2, of which 2 were waited for; matrix products, arithmetic and copies ran while one was open for 11% of the time, Pallas kernels for 0%

profile of v1, /device:TPU:0, one launch (start us, length us, event | category | flops | bytes accessed | tf_op | source)
XLA Modules:
  0.0 345.4 jit_solution(12845587180170388391)
XLA Ops:
  6.5 0.0 copy-start
  6.5 0.0 all-gather.5.cloned.1.call-start
  6.5 5.5 %fusion.10 = bf16[384,4096]{1,0:T(8,128)(2,1)} fusion(bf16[384,4096]{1,0:T(8,128)(2,1)} %param.9), kind=kLoop, calls=%fused_computation.17 | loop fusion | flops 9437184 | bytes 6291456 | tf_op jit(solution)/shard_map/convert_element_type | solution.py:31
  12.0 4.7 %copy.18 = bf16[384,4096]{0,1:T(8,128)(2,1)} copy(bf16[384,4096]{1,0:T(8,128)(2,1)} %fusion.10) | data formatting | bytes 6291456 | tf_op jit(solution)/shard_map/reshape | solution.py:31
  16.7 0.0 copy-done
  16.7 4.2 %fusion.15 = f32[32,128,128]{2,1,0:T(8,128)} fusion(bf16[384,32,128]{0,2,1:T(8,128)(2,1)} %bitcast.59, bf16[384,4096]{1,0:T(8,128)(2,1)S(1)} %copy-done), kind=kOutput, calls=%fused_computation.24 | convolution fusion | flops 402653184 | bytes 8388608 | tf_op jit(solution)/shard_map/thd,the->hde/dot_general | solution.py:33
  20.9 0.0 all-gather.5.cloned.1.call-update
  20.9 0.2 all-gather.7.cloned.1.call-start
  21.2 229.9 %all-gather.5.cloned.1.call-done = f32[256,128,128]{2,1,0:T(8,128)} async-done(((f32[32,128,128]{2,1,0:T(8,128)}), f32[256,128,128]{2,1,0:T(8,128)}) %all-gather.5.cloned.1.call-update) | async-done | bytes 16777232 | tf_op jit(solution)/shard_map/all_gather | solution.py:36
  251.1 9.1 %reduce_sum.18 = f32[32,128,128]{2,1,0:T(8,128)} reduce(f32[8,32,128,128]{3,2,1,0:T(8,128)} %bitcast.56, f32[]{:T(128)} %constant.60.clone.1), dimensions={0}, to_apply=%region_0.1 | reduce | flops 3670016 | bytes 18874372 | tf_op jit(solution)/shard_map/reduce_sum | solution.py:36
  260.2 0.0 all-gather.7.cloned.1.call-update
  260.3 9.2 %fusion = f32[32,384,128]{1,2,0:T(8,128)} fusion(pred[384,384]{1,0:T(8,128)(4,1)S(1)} %iota_compare_fusion, bf16[384,32,128]{0,2,1:T(8,128)(2,1)} %bitcast.60, bf16[384,4096]{1,0:T(8,128)(2,1)S(1)} %copy-done, bf16[384,4096]{1,0:T(8,128)(2,1)} %param.8), kind=kOutput, calls=%fused_computation.3 | convolution fusion | flops 2434793472 | bytes 15876096 | tf_op jit(solution)/shard_map/hts,she->the/dot_general | solution.py:43
  269.5 28.7 %while.29 = (s32[]{:T(128)}, f32[32,128,128]{2,1,0:T(8,128)}, s32[]{:T(128)}, f32[8,32,128,128]{3,2,1,0:T(8,128)}, s32[]{:T(128)}, /*index=5*/s32[]{:T(128)}) while((s32[]{:T(128)}, f32[32,128,128]{2,1,0:T(8,128)}, s32[]{:T(128)}, f32[8,32,128,128]{3,2,1,0:T(8,128)}, s32[]{:T(128)}, /*index=5*/s32[]{:T(128)}) %tuple.71), condition=%wide.region_4.5_spmd.clone, body=%wide.region_3.4_spmd.clone.sunk | while | flops 1572868 | bytes 6291557 | solution.py:19
  269.5 4.1 %add_select_fusion.5 = f32[32,128,128]{2,1,0:T(8,128)} fusion(f32[32,128,128]{2,1,0:T(8,128)} %get-tuple-element.288, f32[8,32,128,128]{3,2,1,0:T(8,128)} %get-tuple-element.296, s32[]{:T(128)S(6)} %copy.48, pred[]{:T(512)S(6)} %compare.7, pred[]{:T(512)S(6)} %lt.43), kind=kLoop, calls=%fused_computation.1.clone.1 | loop fusion | flops 1572864 | bytes 6291462 | tf_op jit(solution)/shard_map/while/body/eval_jaxpr/jit(_where)/select_n | solution.py:17
  273.6 4.1 %add_select_fusion.5 = f32[32,128,128]{2,1,0:T(8,128)} fusion(f32[32,128,128]{2,1,0:T(8,128)} %get-tuple-element.288, f32[8,32,128,128]{3,2,1,0:T(8,128)} %get-tuple-element.296, s32[]{:T(128)S(6)} %copy.48, pred[]{:T(512)S(6)} %compare.7, pred[]{:T(512)S(6)} %lt.43), kind=kLoop, calls=%fused_computation.1.clone.1 | loop fusion | flops 1572864 | bytes 6291462 | tf_op jit(solution)/shard_map/while/body/eval_jaxpr/jit(_where)/select_n | solution.py:17
  277.7 4.1 %add_select_fusion.5 = f32[32,128,128]{2,1,0:T(8,128)} fusion(f32[32,128,128]{2,1,0:T(8,128)} %get-tuple-element.288, f32[8,32,128,128]{3,2,1,0:T(8,128)} %get-tuple-element.296, s32[]{:T(128)S(6)} %copy.48, pred[]{:T(512)S(6)} %compare.7, pred[]{:T(512)S(6)} %lt.43), kind=kLoop, calls=%fused_computation.1.clone.1 | loop fusion | flops 1572864 | bytes 6291462 | tf_op jit(solution)/shard_map/while/body/eval_jaxpr/jit(_where)/select_n | solution.py:17
  281.8 4.2 %add_select_fusion.5 = f32[32,128,128]{2,1,0:T(8,128)} fusion(f32[32,128,128]{2,1,0:T(8,128)} %get-tuple-element.288, f32[8,32,128,128]{3,2,1,0:T(8,128)} %get-tuple-element.296, s32[]{:T(128)S(6)} %copy.48, pred[]{:T(512)S(6)} %compare.7, pred[]{:T(512)S(6)} %lt.43), kind=kLoop, calls=%fused_computation.1.clone.1 | loop fusion | flops 1572864 | bytes 6291462 | tf_op jit(solution)/shard_map/while/body/eval_jaxpr/jit(_where)/select_n | solution.py:17
  286.0 4.1 %add_select_fusion.5 = f32[32,128,128]{2,1,0:T(8,128)} fusion(f32[32,128,128]{2,1,0:T(8,128)} %get-tuple-element.288, f32[8,32,128,128]{3,2,1,0:T(8,128)} %get-tuple-element.296, s32[]{:T(128)S(6)} %copy.48, pred[]{:T(512)S(6)} %compare.7, pred[]{:T(512)S(6)} %lt.43), kind=kLoop, calls=%fused_computation.1.clone.1 | loop fusion | flops 1572864 | bytes 6291462 | tf_op jit(solution)/shard_map/while/body/eval_jaxpr/jit(_where)/select_n | solution.py:17
  290.1 4.1 %add_select_fusion.5 = f32[32,128,128]{2,1,0:T(8,128)} fusion(f32[32,128,128]{2,1,0:T(8,128)} %get-tuple-element.288, f32[8,32,128,128]{3,2,1,0:T(8,128)} %get-tuple-element.296, s32[]{:T(128)S(6)} %copy.48, pred[]{:T(512)S(6)} %compare.7, pred[]{:T(512)S(6)} %lt.43), kind=kLoop, calls=%fused_computation.1.clone.1 | loop fusion | flops 1572864 | bytes 6291462 | tf_op jit(solution)/shard_map/while/body/eval_jaxpr/jit(_where)/select_n | solution.py:17
  294.1 4.1 %add_select_fusion.5 = f32[32,128,128]{2,1,0:T(8,128)} fusion(f32[32,128,128]{2,1,0:T(8,128)} %get-tuple-element.288, f32[8,32,128,128]{3,2,1,0:T(8,128)} %get-tuple-element.296, s32[]{:T(128)S(6)} %copy.48, pred[]{:T(512)S(6)} %compare.7, pred[]{:T(512)S(6)} %lt.43), kind=kLoop, calls=%fused_computation.1.clone.1 | loop fusion | flops 1572864 | bytes 6291462 | tf_op jit(solution)/shard_map/while/body/eval_jaxpr/jit(_where)/select_n | solution.py:17
  298.2 18.6 %all-gather.7.cloned.1.call-done = f32[128,128,128]{2,1,0:T(8,128)} async-done(((f32[32,128,128]{2,1,0:T(8,128)}), f32[128,128,128]{2,1,0:T(8,128)}) %all-gather.7.cloned.1.call-update) | async-done | bytes 8388624 | tf_op jit(solution)/shard_map/all_gather | solution.py:12
  316.8 0.0 copy-done.2
  316.8 7.0 %while.28 = (s32[]{:T(128)}, f32[32,128,128]{2,1,0:T(8,128)S(1)}, s32[]{:T(128)}, f32[4,32,128,128]{3,2,1,0:T(8,128)}, s32[]{:T(128)}, /*index=5*/s32[]{:T(128)}) while((s32[]{:T(128)}, f32[32,128,128]{2,1,0:T(8,128)S(1)}, s32[]{:T(128)}, f32[4,32,128,128]{3,2,1,0:T(8,128)}, s32[]{:T(128)}, /*index=5*/s32[]{:T(128)}) %tuple.72), condition=%wide.region_2.3_spmd.clone, body=%wide.region_1.2_spmd.clone.sunk | while | flops 1572868 | bytes 6291557 | solution.py:19
  316.8 2.3 add_select_fusion.4
  319.1 2.3 add_select_fusion.4
  321.5 2.3 add_select_fusion.4
  323.8 0.0 slice-start
  323.8 0.0 slice-start.1
  323.8 7.4 %multiply_reduce_fusion = (f32[384,32]{0,1:T(8,128)S(1)}, f32[32,128,384]{2,1,0:T(8,128)S(1)}) fusion(f32[32,384,128]{1,2,0:T(8,128)} %fusion, f32[32,128,128]{2,1,0:T(8,128)S(1)} %get-tuple-element.163, f32[32,128,128]{2,1,0:T(8,128)} %get-tuple-element.164, bf16[384,4096]{1,0:T(8,128)(2,1)} %param.8), kind=kOutput, calls=%fused_computation.20 | convolution fusion | flops 417845248 | bytes 19972096 | tf_op jit(solution)/shard_map/thd,hde->the/dot_general | solution.py:44
  331.3 2.5 multiply_convert_fusion
  333.8 4.8 %copy.16 = bf16[384,4096]{1,0:T(8,128)(2,1)} copy(bf16[384,4096]{0,1:T(8,128)(2,1)} %bitcast.61) | data formatting | bytes 6291456 | tf_op jit(solution)/shard_map/convert_element_type | solution.py:51
  338.6 0.0 copy-done.1
  (12 shorter events, 0.1 us)
Async XLA Ops:
  6.5 10.2 %copy-start = (bf16[384,4096]{1,0:T(8,128)(2,1)S(1)}, bf16[384,4096]{1,0:T(8,128)(2,1)}, u32[]{:S(2)}) copy-start(bf16[384,4096]{1,0:T(8,128)(2,1)} %param.10) | copy-start | bytes 9437188
  6.5 244.6 %all-gather.5.cloned.1.call-start = ((), (), s32[]{:S(2)}) async-start(), calls=%async_computation | async-start | bytes 18874368 | tf_op jit(solution)/shard_map/all_gather | solution.py:36
  20.9 295.9 %all-gather.7.cloned.1.call-start = ((), (), s32[]{:S(2)}) async-start(), calls=%async_computation.1 | async-start | bytes 10485760 | tf_op jit(solution)/shard_map/all_gather | solution.py:12
  251.1 9.2 %copy-start.3 = (bf16[4096]{0:T(1024)(128)(2,1)S(1)}, bf16[4096]{0:T(1024)(128)(2,1)}, u32[]{:S(2)}) copy-start(bf16[4096]{0:T(1024)(128)(2,1)} %param.11) | copy-start | bytes 24580
  269.5 47.3 %copy-start.2 = (f32[32,128,128]{2,1,0:T(8,128)S(1)}, f32[32,128,128]{2,1,0:T(8,128)}, u32[]{:S(2)}) copy-start(f32[32,128,128]{2,1,0:T(8,128)} %custom-call) | copy-start | bytes 6291460
  323.8 7.5 %slice-start = ((s8[6291456]{0:T(1024)(128)(4,1)}), s8[4194304]{0:T(1024)(128)(4,1)S(1)}, s32[]{:S(2)}) async-start(s8[6291456]{0:T(1024)(128)(4,1)} %bitcast.62), calls=%async_computation.2 | async-start | bytes 8388608
  323.8 7.5 %slice-start.1 = ((s8[6291456]{0:T(1024)(128)(4,1)}), s8[2097152]{0:T(1024)(128)(4,1)S(1)}, s32[]{:S(2)}) async-start(s8[6291456]{0:T(1024)(128)(4,1)} %bitcast.62), calls=%async_computation.3 | async-start | bytes 4194304
  333.8 4.8 %copy-start.1 = (bf16[384,4096]{1,0:T(8,128)(2,1)S(1)}, bf16[384,4096]{1,0:T(8,128)(2,1)}, u32[]{:S(2)}) copy-start(bf16[384,4096]{1,0:T(8,128)(2,1)} %param.10) | copy-start | bytes 9437188
Sparse Core Ops, SparseCore 0:
  21.1 229.9 all-gather.4
  260.3 56.4 all-gather.6
